TPU v7x, 32 devices: a whole 2x2x4 slice. The times are simulated.
32 devices in a mesh: clip: 2 (over x), frame: 8 (over z, y), band: 2 (over core).
Axes of the slice: x: 2, y: 2, z: 4, core: 2. Of those that a mesh axis runs over, the one named last changes fastest.
Arguments:
- pixels: bfloat16 [16, 16, 32, 256], P(('clip', 'frame'), 'band'), parts along dimension 0, may hold values from -40 to 40
- gru_state: bfloat16 [16, 16, 32, 128], P(('clip', 'frame'), 'band'), parts along dimension 0, may hold values from -1 to 1
- tokens: bfloat16 [16, 1024, 256], P(('clip', 'frame'), 'band'), parts along dimension 0, may hold values from -30 to 30
- visible: int32 [16, 1024], P(('clip', 'frame'), 'band'), parts along dimension 0, may hold values from 0 to 1, as said below
- query_frame: int32 [2048], P(('clip', 'band')), parts along dimension 0, may hold values from 0 to 7, as said below
- pixel_query: bfloat16 [256, 256], replicated, may hold values from -2 to 2
- pixel_key: bfloat16 [256, 256], replicated, may hold values from -2 to 2
- pixel_value: bfloat16 [256, 256], replicated, may hold values from -0.375 to 0.375
- pixel_out: bfloat16 [256, 128], replicated, may hold values from -1.5 to 1.5
- time_query: bfloat16 [256, 256], replicated, may hold values from -2 to 2
- time_key: bfloat16 [256, 256], replicated, may hold values from -2 to 2
- time_value: bfloat16 [256, 256], replicated, may hold values from -0.375 to 0.375
- time_out: bfloat16 [256, 256], replicated, may hold values from -0.75 to 0.75
- gru_gates: bfloat16 [3, 3, 256, 256], replicated, may hold values from -0.125 to 0.125
- gru_candidate: bfloat16 [3, 3, 256, 128], replicated, may hold values from -0.125 to 0.125
Outputs:
- refined_state: bfloat16 [16, 16, 32, 128], P(('clip', 'frame'), 'band'), parts along dimension 0
- track_out: bfloat16 [16, 1024, 256], P(('clip', 'frame'), 'band'), parts along dimension 0
There are 2 independent parts, one for each index of `clip`. A program takes and returns all parts, laid end to end along the dimension named above; an argument that names none is the same for every part. Nothing has to cross between parts.
Inputs may be any that keep to these rules, and one draw needn't show every extreme that they name: Each track is visible in the frame named by its query frame index. `query_frame`: every frame is the query frame of exactly 128 tracks.
All inputs are finite; a program needn't handle non-finite values.
Results may differ from a plain program's by a relative error of at most 0.0095.
The roundings to bfloat16 on the way count: a program that leaves them out, or rounds other values in their place, can miss the bound.
Values may be sent and summed in bfloat16 or wider, within the bound.
A program may use at most 64 MiB of HBM per device.

v0:
```python
import jax
import jax.numpy as jnp
from jax import lax
from jax.sharding import PartitionSpec as P

HEADS = 8
HEAD_DIM = 32
GRU_WIDTH = 128
ITERS = 2


def with_halo(x, sides, width):
    for axis, dim in sides:
        devices, length = (lax.axis_size(axis), x.shape[dim])
        up = [(i, (i + 1) % devices) for i in range(devices - 1)]
        down = [(j, i) for i, j in up]
        last = lax.slice_in_dim(x, length - width, length, axis=dim)
        first = lax.slice_in_dim(x, 0, width, axis=dim)
        before = lax.ppermute(last, axis, up)
        after = lax.ppermute(first, axis, down)
        x = jnp.concatenate([before, x, after], axis=dim)
    return x


def attend_heads(queries, key_rows, value_rows, key_mask):
    score_scale = HEAD_DIM ** (-0.5)
    head_outputs = []
    for head_index in range(HEADS):
        offset = head_index * HEAD_DIM
        scores = (
            jnp.dot(
                queries[:, offset : offset + HEAD_DIM],
                key_rows[:, offset : offset + HEAD_DIM].T,
                preferred_element_type=jnp.float32,
            )
            * score_scale
        )
        scores = jnp.where(key_mask[None, :], scores, -jnp.inf)
        weights = jax.nn.softmax(scores, axis=-1).astype(jnp.bfloat16)
        head_outputs.append(
            jnp.dot(
                weights,
                value_rows[:, offset : offset + HEAD_DIM],
                preferred_element_type=jnp.float32,
            )
        )
    return jnp.concatenate(head_outputs, axis=-1).astype(jnp.bfloat16)


def conv_rows(padded, weight, rows, columns):
    widened = jnp.pad(padded, ((0, 0), (1, 1), (0, 0)))
    summed = jnp.zeros((rows * columns, weight.shape[3]), jnp.float32)
    for row_shift in range(3):
        for col_shift in range(3):
            window = widened[row_shift : row_shift + rows, col_shift : col_shift + columns]
            summed = summed + jnp.dot(
                window.reshape(rows * columns, -1),
                weight[row_shift, col_shift],
                preferred_element_type=jnp.float32,
            )
    return summed


def temporal_core(query_part, key_part, value_part, seen_part, anchor_part):
    frames_here, track_count, channels = query_part.shape
    anchor = jnp.einsum("fk,fkc->kc", anchor_part, query_part, preferred_element_type=jnp.float32)
    joint_query = (query_part.astype(jnp.float32) + anchor[None]).astype(jnp.bfloat16)
    shaped = (frames_here, track_count, HEADS, HEAD_DIM)
    scores = jnp.einsum(
        "fkhd,gkhd->khfg",
        joint_query.reshape(shaped),
        key_part.reshape(shaped),
        preferred_element_type=jnp.float32,
    ) * HEAD_DIM ** (-0.5)
    key_mask = jnp.transpose(seen_part) > 0
    scores = jnp.where(key_mask[:, None, None, :], scores, -jnp.inf)
    weights = jax.nn.softmax(scores, axis=-1).astype(jnp.bfloat16)
    attended = jnp.einsum(
        "khfg,gkhd->fkhd", weights, value_part.reshape(shaped), preferred_element_type=jnp.float32
    )
    return attended.astype(jnp.bfloat16).reshape(frames_here, track_count, channels)


def on_device(
    pixels,
    gru_state,
    tokens,
    visible,
    query_frame,
    pixel_query,
    pixel_key,
    pixel_value,
    pixel_out,
    time_query,
    time_key,
    time_value,
    time_out,
    gru_gates,
    gru_candidate,
):
    frame_pos = lax.axis_index("frame")
    frames = lax.axis_size("frame")
    channels = tokens.shape[2]
    half_tracks = tokens.shape[1]
    per_device = half_tracks // frames
    band_rows = pixels.shape[1]
    columns = pixels.shape[2]
    local_tokens = tokens[0]
    seen_mask = visible[0].astype(jnp.bfloat16)
    anchor_mask = (query_frame == frame_pos).astype(jnp.bfloat16)
    seen_split = seen_mask.reshape(1, frames, per_device)
    anchor_split = anchor_mask.reshape(1, frames, per_device)
    token_part = lax.all_to_all(
        local_tokens.reshape(1, frames, per_device, channels),
        "frame",
        split_axis=1,
        concat_axis=0,
        tiled=True,
    )
    seen_part = lax.all_to_all(seen_split, "frame", split_axis=1, concat_axis=0, tiled=True)
    anchor_part = lax.all_to_all(anchor_split, "frame", split_axis=1, concat_axis=0, tiled=True)
    token_rows = token_part[:, 0]
    frames_here, track_count, width_here = token_rows.shape
    flat_rows = token_rows.reshape(frames_here * track_count, width_here)
    outputs = []
    for weight in (time_query, time_key, time_value):
        outputs.append(
            jnp.dot(flat_rows, weight, preferred_element_type=jnp.float32)
            .astype(jnp.bfloat16)
            .reshape(frames_here, track_count, width_here)
        )
    result = temporal_core(outputs[0], outputs[1], outputs[2], seen_part[:, 0], anchor_part[:, 0])
    track_result = result[:, None]
    flat_pixels = pixels[0].reshape(band_rows * columns, channels)
    queries = jnp.dot(flat_pixels, pixel_query, preferred_element_type=jnp.float32).astype(
        jnp.bfloat16
    )
    key_local = jnp.dot(local_tokens, pixel_key, preferred_element_type=jnp.float32).astype(
        jnp.bfloat16
    )
    value_local = jnp.dot(local_tokens, pixel_value, preferred_element_type=jnp.float32).astype(
        jnp.bfloat16
    )
    key_rows, value_rows, seen_all = (
        lax.all_gather(key_local, "band", axis=0, tiled=True),
        lax.all_gather(value_local, "band", axis=0, tiled=True),
        lax.all_gather(seen_mask, "band", axis=0, tiled=True),
    )
    attended = attend_heads(queries, key_rows, value_rows, seen_all > 0)
    context = (
        jnp.dot(attended, pixel_out, preferred_element_type=jnp.float32)
        .astype(jnp.bfloat16)
        .reshape(band_rows, columns, GRU_WIDTH)
    )
    returned = lax.all_to_all(track_result, "frame", split_axis=0, concat_axis=1, tiled=True)
    returned_rows = returned.reshape(half_tracks, channels)
    track_update = jnp.dot(returned_rows, time_out, preferred_element_type=jnp.float32)
    track_out = (local_tokens.astype(jnp.float32) + track_update).astype(jnp.bfloat16)[None]
    state_now = gru_state[0]
    for iteration in range(ITERS):
        combined = jnp.concatenate([state_now, context], axis=-1)
        padded = with_halo(combined, (("band", 0),), 1)
        gate_terms = conv_rows(padded, gru_gates, band_rows, columns)
        update = jax.nn.sigmoid(gate_terms[:, :GRU_WIDTH])
        reset_gate = jax.nn.sigmoid(gate_terms[:, GRU_WIDTH:])
        state_flat = state_now.reshape(band_rows * columns, GRU_WIDTH).astype(jnp.float32)
        reset_state = (
            (reset_gate * state_flat).astype(jnp.bfloat16).reshape(band_rows, columns, GRU_WIDTH)
        )
        mixed_in = jnp.concatenate([reset_state, context], axis=-1)
        padded_mix = with_halo(mixed_in, (("band", 0),), 1)
        candidate = jnp.tanh(conv_rows(padded_mix, gru_candidate, band_rows, columns))
        state_now = (
            ((1.0 - update) * state_flat + update * candidate)
            .astype(jnp.bfloat16)
            .reshape(band_rows, columns, GRU_WIDTH)
        )
    refined_state = state_now[None]
    return (refined_state, track_out)


def solution(mesh):
    placed = (
        P(("clip", "frame"), "band", None, None),
        P(("clip", "frame"), "band", None, None),
        P(("clip", "frame"), "band", None),
        P(("clip", "frame"), "band"),
        P(("clip", "band")),
        P(),
        P(),
        P(),
        P(),
        P(),
        P(),
        P(),
        P(),
        P(),
        P(),
    )
    return jax.shard_map(
        on_device,
        mesh=mesh,
        in_specs=placed,
        out_specs=(P(("clip", "frame"), "band", None, None), P(("clip", "frame"), "band", None)),
        check_vma=False,
    )
```

profile of v0, /device:TPU:0, one launch (start us, length us, event | category | flops | bytes accessed | tf_op | source)
XLA Modules:
  0.0 105.7 jit_solution(6565268605685878097)
XLA Ops:
  0.7 0.9 copy-done
  1.5 1.2 %convolution_convert_fusion.5 = bf16[512,256]{1,0:T(8,128)(2,1)S(1)} fusion(bf16[256,256]{1,0:T(8,128)(2,1)S(1)} %copy-done, bf16[1,512,256]{2,1,0:T(8,128)(2,1)} %param.17), kind=kOutput, calls=%fused_computation.25 | convolution fusion | flops 67239936 | bytes 655360 | tf_op jit(solution)/shard_map/dot_general | solution.py:138
  2.7 2.3 %all_gather.10 = bf16[1024,256]{1,0:T(8,128)(2,1)S(1)} all-gather(bf16[512,256]{1,0:T(8,128)(2,1)S(1)} %convolution_convert_fusion.5), channel_id=1, replica_groups=mesh['clip'=2,'frame'=8,'band'=2] {'band'}, dimensions={0}, use_global_device_ids=true | all-gather | bytes 786432 | tf_op jit(solution)/shard_map/all_gather | solution.py:145
  5.0 1.9 %all-gather = bf16[1,1024]{1,0:T(2,128)(2,1)S(1)} all-gather(bf16[1,512]{1,0:T(2,128)(2,1)S(1)} %convert_element_type.112), channel_id=2, replica_groups=mesh['clip'=2,'frame'=8,'band'=2] {'band'}, dimensions={1}, use_global_device_ids=true | all-gather | bytes 3072 | tf_op jit(solution)/shard_map/all_gather | solution.py:147
  7.6 0.5 fusion.197
  8.1 0.5 fusion.198
  8.6 0.5 fusion.199
  9.5 0.5 fusion.201
  10.0 0.5 fusion.202
  10.4 0.5 fusion.203
  10.9 1.2 %convolution_convert_fusion.4 = bf16[512,256]{1,0:T(8,128)(2,1)S(1)} fusion(bf16[256,256]{1,0:T(8,128)(2,1)S(1)} %copy-done.11, bf16[1,512,256]{2,1,0:T(8,128)(2,1)} %param.17), kind=kOutput, calls=%fused_computation.24 | convolution fusion | flops 67239936 | bytes 655360 | tf_op jit(solution)/shard_map/dot_general | solution.py:141
  12.1 2.2 %all_gather.11 = bf16[1024,256]{1,0:T(8,128)(2,1)S(1)} all-gather(bf16[512,256]{1,0:T(8,128)(2,1)S(1)} %convolution_convert_fusion.4), channel_id=1, replica_groups=mesh['clip'=2,'frame'=8,'band'=2] {'band'}, dimensions={0}, use_global_device_ids=true | all-gather | bytes 786432 | tf_op jit(solution)/shard_map/all_gather | solution.py:146
  15.3 0.5 fusion.32
  16.9 0.5 fusion.30
  21.1 2.4 %collective-permute-start = (bf16[1,32,256]{2,1,0:T(8,128)(2,1)S(1)}, bf16[1,32,256]{2,1,0:T(8,128)(2,1)S(1)}, u32[]{:S(2)}, u32[]{:S(2)}) collective-permute-start(bf16[1,32,256]{2,1,0:T(8,128)(2,1)S(1)} %get-tuple-element.42), channel_id=1, source_target_pairs={{0,1},{2,3},{4,5},{6,7},{8,9},{10,11},{12,13},{14,15},{16,17},{18,... | collective-permute-start | bytes 49160 | tf_op jit(solution)/shard_map/ppermute | solution.py:19
  23.5 1.3 %collective-permute-start.1 = (bf16[1,32,256]{2,1,0:T(8,128)(2,1)S(1)}, bf16[1,32,256]{2,1,0:T(8,128)(2,1)S(1)}, u32[]{:S(2)}, u32[]{:S(2)}) collective-permute-start(bf16[1,32,256]{2,1,0:T(8,128)(2,1)S(1)} %get-tuple-element.2), channel_id=1, source_target_pairs={{1,0},{3,2},{5,4},{7,6},{9,8},{11,10},{13,12},{15,14},{17,16},{19,... | collective-permute-start | bytes 49160 | tf_op jit(solution)/shard_map/ppermute | solution.py:20
  24.8 0.7 reshape.250
  25.5 7.0 %all-to-all-start.2 = ((bf16[1,8,64]{2,0,1:T(2,128)(2,1)}), bf16[1,8,64]{2,0,1:T(2,128)(2,1)S(1)}, u32[]{:S(2)}, u32[]{:S(2)}) async-start(bf16[1,8,64]{2,0,1:T(2,128)(2,1)} %reshape.250), calls=%async_computation.2 | async-start | bytes 8192 | tf_op jit(solution)/shard_map/all_to_all | solution.py:121
  34.5 2.7 %collective-permute-start.2 = (bf16[1,32,256]{2,1,0:T(8,128)(2,1)S(1)}, bf16[1,32,256]{2,1,0:T(8,128)(2,1)S(1)}, u32[]{:S(2)}, u32[]{:S(2)}) collective-permute-start(bf16[1,32,256]{2,1,0:T(8,128)(2,1)S(1)} %get-tuple-element.40), channel_id=1, source_target_pairs={{0,1},{2,3},{4,5},{6,7},{8,9},{10,11},{12,13},{14,15},{16,17},{18,... | collective-permute-start | bytes 49160 | tf_op jit(solution)/shard_map/ppermute | solution.py:19
  37.2 1.3 %collective-permute-start.3 = (bf16[1,32,256]{2,1,0:T(8,128)(2,1)S(1)}, bf16[1,32,256]{2,1,0:T(8,128)(2,1)S(1)}, u32[]{:S(2)}, u32[]{:S(2)}) collective-permute-start(bf16[1,32,256]{2,1,0:T(8,128)(2,1)S(1)} %get-tuple-element.41), channel_id=1, source_target_pairs={{1,0},{3,2},{5,4},{7,6},{9,8},{11,10},{13,12},{15,14},{17,16},{19,... | collective-permute-start | bytes 49160 | tf_op jit(solution)/shard_map/ppermute | solution.py:20
  38.5 0.7 convert_element_type.145
  39.2 1.1 %collective-permute-done.3 = bf16[1,32,256]{2,1,0:T(8,128)(2,1)S(1)} collective-permute-done((bf16[1,32,256]{2,1,0:T(8,128)(2,1)S(1)}, bf16[1,32,256]{2,1,0:T(8,128)(2,1)S(1)}, u32[]{:S(2)}, u32[]{:S(2)}) %collective-permute-start.3) | collective-permute-done | bytes 16416 | tf_op jit(solution)/shard_map/ppermute | solution.py:20
  42.1 2.1 %collective-permute-start.4 = (bf16[1,32,256]{2,1,0:T(8,128)(2,1)S(1)}, bf16[1,32,256]{2,1,0:T(8,128)(2,1)S(1)}, u32[]{:S(2)}, u32[]{:S(2)}) collective-permute-start(bf16[1,32,256]{2,1,0:T(8,128)(2,1)S(1)} %get-tuple-element.38), channel_id=1, source_target_pairs={{0,1},{2,3},{4,5},{6,7},{8,9},{10,11},{12,13},{14,15},{16,17},{18,... | collective-permute-start | bytes 49160 | tf_op jit(solution)/shard_map/ppermute | solution.py:19
  44.2 1.3 %collective-permute-start.5 = (bf16[1,32,256]{2,1,0:T(8,128)(2,1)S(1)}, bf16[1,32,256]{2,1,0:T(8,128)(2,1)S(1)}, u32[]{:S(2)}, u32[]{:S(2)}) collective-permute-start(bf16[1,32,256]{2,1,0:T(8,128)(2,1)S(1)} %get-tuple-element.39), channel_id=1, source_target_pairs={{1,0},{3,2},{5,4},{7,6},{9,8},{11,10},{13,12},{15,14},{17,16},{19,... | collective-permute-start | bytes 49160 | tf_op jit(solution)/shard_map/ppermute | solution.py:20
  45.5 5.7 %all-to-all-start.1 = ((bf16[1,8,64]{2,0,1:T(2,128)(2,1)}), bf16[1,8,64]{2,0,1:T(2,128)(2,1)S(1)}, u32[]{:S(2)}, u32[]{:S(2)}) async-start(bf16[1,8,64]{2,0,1:T(2,128)(2,1)} %convert_element_type.145), calls=%async_computation.1 | async-start | bytes 8192 | tf_op jit(solution)/shard_map/all_to_all | solution.py:120
  53.2 0.6 copy-done.6
  53.9 2.7 %collective-permute-start.6 = (bf16[1,32,256]{2,1,0:T(8,128)(2,1)S(1)}, bf16[1,32,256]{2,1,0:T(8,128)(2,1)S(1)}, u32[]{:S(2)}, u32[]{:S(2)}) collective-permute-start(bf16[1,32,256]{2,1,0:T(8,128)(2,1)S(1)} %get-tuple-element.36), channel_id=1, source_target_pairs={{0,1},{2,3},{4,5},{6,7},{8,9},{10,11},{12,13},{14,15},{16,17},{18,... | collective-permute-start | bytes 49160 | tf_op jit(solution)/shard_map/ppermute | solution.py:19
  56.6 1.3 %collective-permute-start.7 = (bf16[1,32,256]{2,1,0:T(8,128)(2,1)S(1)}, bf16[1,32,256]{2,1,0:T(8,128)(2,1)S(1)}, u32[]{:S(2)}, u32[]{:S(2)}) collective-permute-start(bf16[1,32,256]{2,1,0:T(8,128)(2,1)S(1)} %get-tuple-element.37), channel_id=1, source_target_pairs={{1,0},{3,2},{5,4},{7,6},{9,8},{11,10},{13,12},{15,14},{17,16},{19,... | collective-permute-start | bytes 49160 | tf_op jit(solution)/shard_map/ppermute | solution.py:20
  58.0 5.7 %all-to-all-start = ((bf16[1,8,64,256]{3,2,0,1:T(8,128)(2,1)}), bf16[1,8,64,256]{3,2,0,1:T(8,128)(2,1)S(1)}, u32[]{:S(2)}, u32[]{:S(2)}) async-start(bf16[1,8,64,256]{3,2,0,1:T(8,128)(2,1)} %bitcast.61), calls=%async_computation | async-start | bytes 524288 | tf_op jit(solution)/shard_map/all_to_all | solution.py:113
  63.7 0.8 pad_slice_fusion.1
  64.7 0.7 fusion.78
  66.2 0.8 convolution_add_fusion.16
  67.1 6.8 %all-to-all-done = bf16[1,8,64,256]{3,2,0,1:T(8,128)(2,1)S(1)} async-done(((bf16[1,8,64,256]{3,2,0,1:T(8,128)(2,1)}), bf16[1,8,64,256]{3,2,0,1:T(8,128)(2,1)S(1)}, u32[]{:S(2)}, u32[]{:S(2)}) %all-to-all-start) | async-done | bytes 262176 | tf_op jit(solution)/shard_map/all_to_all | solution.py:113
  74.8 1.8 %copy.70 = bf16[8,64,8,32]{3,0,2,1:T(8,128)(2,1)S(1)} copy(bf16[8,64,8,32]{1,0,3,2:T(8,128)(2,1)S(1)} %add_convert_fusion) | data formatting | bytes 524288 | tf_op jit(solution)/shard_map/convert_element_type | solution.py:67
  77.2 2.7 %copy.71 = bf16[8,64,8,32]{3,0,2,1:T(8,128)(2,1)} copy(bf16[8,64,8,32]{1,0,3,2:T(8,128)(2,1)S(1)} %reshape_reshape.7) | data formatting | bytes 524288 | tf_op jit(solution)/shard_map/reshape;reshape | solution.py:72
  79.9 1.9 %fusion.205 = f32[64,8,8,8]{2,3,1,0:T(8,128)S(1)} fusion(bf16[8,64,8,32]{3,0,2,1:T(8,128)(2,1)S(1)} %copy.70, bf16[8,64,8,32]{3,0,2,1:T(8,128)(2,1)} %copy.71), kind=kOutput, calls=%fused_computation.340 | convolution fusion | flops 2097152 | bytes 655360 | tf_op jit(solution)/shard_map/fkhd,gkhd->khfg/dot_general | solution.py:69
  81.9 1.1 %copy.72 = f32[64,8,8,8]{0,3,2,1:T(8,128)S(1)} copy(f32[64,8,8,8]{2,3,1,0:T(8,128)S(1)} %fusion.205) | data formatting | bytes 262144 | tf_op jit(solution)/shard_map/fkhd,gkhd->khfg/dot_general | solution.py:69
  83.0 1.2 %fusion.204 = (f32[64,8,8]{0,2,1:T(8,128)S(1)}, f32[64,8,8,8]{0,3,2,1:T(8,128)S(1)}) fusion(f32[64,8,8,8]{0,3,2,1:T(8,128)S(1)} %copy.72, pred[64,8]{0,1:T(8,128)(4,1)S(1)} %compare_bitcast_fusion), kind=kOutput, calls=%fused_computation.339 | output fusion | flops 131079 | bytes 279040 | tf_op jit(solution)/shard_map/sub | solution.py:77
  84.2 1.6 %copy.74 = bf16[64,8,8,8]{3,2,1,0:T(8,128)(2,1)S(1)} copy(bf16[64,8,8,8]{0,3,2,1:T(8,128)(2,1)S(1)} %divide_convert_fusion.16) | data formatting | bytes 131072 | tf_op jit(solution)/shard_map/convert_element_type | solution.py:77
  86.5 1.8 %copy.73 = bf16[8,64,8,32]{3,0,2,1:T(8,128)(2,1)S(1)} copy(bf16[8,64,8,32]{1,0,3,2:T(8,128)(2,1)S(1)} %reshape_reshape.6) | data formatting | bytes 524288 | tf_op jit(solution)/shard_map/reshape;reshape | solution.py:79
  88.2 0.7 fusion.1
  88.9 1.2 %copy.75 = bf16[8,64,8,32]{1,3,2,0:T(8,128)(2,1)S(1)} copy(bf16[8,64,8,32]{3,0,2,1:T(8,128)(2,1)S(1)} %fusion.1) | data formatting | bytes 524288 | tf_op jit(solution)/shard_map/convert_element_type | solution.py:81
  90.1 0.9 copy.76
  91.0 3.6 %all-to-all-start.3 = ((bf16[8,1,64,256]{3,2,1,0:T(8,128)(2,1)}), bf16[8,1,64,256]{3,2,1,0:T(8,128)(2,1)S(1)}, u32[]{:S(2)}, u32[]{:S(2)}) async-start(bf16[8,1,64,256]{3,2,1,0:T(8,128)(2,1)} %copy.76), calls=%async_computation.3 | async-start | bytes 524288 | tf_op jit(solution)/shard_map/all_to_all | solution.py:155
  94.7 1.0 fusion.138
  95.7 1.7 %fusion.24 = bf16[256,128]{1,0:T(8,128)(2,1)} fusion(f32[256,128]{1,0:T(8,128)S(1)} %fusion.138, f32[256,128]{1,0:T(8,128)S(1)} %copy-done.16, bf16[256,256]{1,0:T(8,128)(2,1)S(1)} %bitcast.277, bf16[256,128]{1,0:T(8,128)(2,1)S(1)} %copy-done.5, f32[256,256]{1,0:T(8,128)S(1)} %copy-done.7, bf16[3,3,256,128]{3,2,1,0:T(8,128)(2,1)} %param.29), kind=kOutput, calls=%fused_computation.68 | convolution fusion | flops 17137664 | bytes 720896 | tf_op jit(solution)/shard_map/dot_general | solution.py:56
  97.4 6.5 %all-to-all-done.3 = bf16[8,1,64,256]{3,2,1,0:T(8,128)(2,1)S(1)} async-done(((bf16[8,1,64,256]{3,2,1,0:T(8,128)(2,1)}), bf16[8,1,64,256]{3,2,1,0:T(8,128)(2,1)S(1)}, u32[]{:S(2)}, u32[]{:S(2)}) %all-to-all-start.3) | async-done | bytes 262176 | tf_op jit(solution)/shard_map/all_to_all | solution.py:155
  103.9 1.9 %fusion.12 = bf16[1,512,256]{2,1,0:T(8,128)(2,1)} fusion(bf16[512,256]{1,0:T(8,128)(2,1)S(1)} %bitcast.244, bf16[256,256]{1,0:T(8,128)(2,1)S(1)} %copy-done.15, bf16[1,512,256]{2,1,0:T(8,128)(2,1)} %param.17), kind=kOutput, calls=%fused_computation.27 | convolution fusion | flops 67502080 | bytes 917504 | tf_op jit(solution)/shard_map/dot_general | solution.py:157
  (135 shorter events, 15.7 us)
Async XLA Ops:
  0.6 0.9 copy-start
  0.6 4.4 %copy-start.19 = (s32[1,512]{1,0:T(1,128)S(1)}, s32[1,512]{1,0:T(1,128)}, u32[]{:S(2)}) copy-start(s32[1,512]{1,0:T(1,128)} %param.18) | copy-start | bytes 6148
  0.7 6.3 %copy-start.9 = (bf16[1,8,32,256]{3,2,1,0:T(8,128)(2,1)S(1)}, bf16[1,8,32,256]{3,2,1,0:T(8,128)(2,1)}, u32[]{:S(2)}) copy-start(bf16[1,8,32,256]{3,2,1,0:T(8,128)(2,1)} %param.15) | copy-start | bytes 393220
  0.7 6.3 %copy-start.10 = (bf16[256,256]{1,0:T(8,128)(2,1)S(1)}, bf16[256,256]{1,0:T(8,128)(2,1)}, u32[]{:S(2)}) copy-start(bf16[256,256]{1,0:T(8,128)(2,1)} %param.20) | copy-start | bytes 393220
  9.9 1.0 copy-start.11
  20.0 0.8 copy-start.18
  20.0 1.1 %copy-start.3 = (bf16[1,8,32,128]{3,2,1,0:T(8,128)(2,1)S(1)}, bf16[1,8,32,128]{3,2,1,0:T(8,128)(2,1)}, u32[]{:S(2)}) copy-start(bf16[1,8,32,128]{3,2,1,0:T(8,128)(2,1)} %param.16) | copy-start | bytes 196612
  20.0 4.8 %copy-start.20 = (s32[512]{0:T(512)S(1)}, s32[512]{0:T(512)}, u32[]{:S(2)}) copy-start(s32[512]{0:T(512)} %param.19) | copy-start | bytes 6148
  20.8 11.8 %copy-start.1 = (bf16[3,3,256,256]{3,2,1,0:T(8,128)(2,1)S(1)}, bf16[3,3,256,256]{3,2,1,0:T(8,128)(2,1)}, u32[]{:S(2)}) copy-start(bf16[3,3,256,256]{3,2,1,0:T(8,128)(2,1)} %param.28) | copy-start | bytes 3538948
  21.1 11.4 %collective-permute-start = (bf16[1,32,256]{2,1,0:T(8,128)(2,1)S(1)}, bf16[1,32,256]{2,1,0:T(8,128)(2,1)S(1)}, u32[]{:S(2)}, u32[]{:S(2)}) collective-permute-start(bf16[1,32,256]{2,1,0:T(8,128)(2,1)S(1)} %get-tuple-element.42), channel_id=1, source_target_pairs={{0,1},{2,3},{4,5},{6,7},{8,9},{10,11},{12,13},{14,15},{16,17},{18,... | collective-permute-start | bytes 49160 | tf_op jit(solution)/shard_map/ppermute | solution.py:19
  23.5 9.0 %collective-permute-start.1 = (bf16[1,32,256]{2,1,0:T(8,128)(2,1)S(1)}, bf16[1,32,256]{2,1,0:T(8,128)(2,1)S(1)}, u32[]{:S(2)}, u32[]{:S(2)}) collective-permute-start(bf16[1,32,256]{2,1,0:T(8,128)(2,1)S(1)} %get-tuple-element.2), channel_id=1, source_target_pairs={{1,0},{3,2},{5,4},{7,6},{9,8},{11,10},{13,12},{15,14},{17,16},{19,... | collective-permute-start | bytes 49160 | tf_op jit(solution)/shard_map/ppermute | solution.py:20
  25.5 20.0 %all-to-all-start.2 = ((bf16[1,8,64]{2,0,1:T(2,128)(2,1)}), bf16[1,8,64]{2,0,1:T(2,128)(2,1)S(1)}, u32[]{:S(2)}, u32[]{:S(2)}) async-start(bf16[1,8,64]{2,0,1:T(2,128)(2,1)} %reshape.250), calls=%async_computation.2 | async-start | bytes 8192 | tf_op jit(solution)/shard_map/all_to_all | solution.py:121
  34.2 6.3 %copy-start.2 = (bf16[3,3,256,128]{3,2,1,0:T(8,128)(2,1)S(1)}, bf16[3,3,256,128]{3,2,1,0:T(8,128)(2,1)}, u32[]{:S(2)}) copy-start(bf16[3,3,256,128]{3,2,1,0:T(8,128)(2,1)} %param.29) | copy-start | bytes 1769476
  34.5 4.8 %collective-permute-start.2 = (bf16[1,32,256]{2,1,0:T(8,128)(2,1)S(1)}, bf16[1,32,256]{2,1,0:T(8,128)(2,1)S(1)}, u32[]{:S(2)}, u32[]{:S(2)}) collective-permute-start(bf16[1,32,256]{2,1,0:T(8,128)(2,1)S(1)} %get-tuple-element.40), channel_id=1, source_target_pairs={{0,1},{2,3},{4,5},{6,7},{8,9},{10,11},{12,13},{14,15},{16,17},{18,... | collective-permute-start | bytes 49160 | tf_op jit(solution)/shard_map/ppermute | solution.py:19
  37.2 3.1 %collective-permute-start.3 = (bf16[1,32,256]{2,1,0:T(8,128)(2,1)S(1)}, bf16[1,32,256]{2,1,0:T(8,128)(2,1)S(1)}, u32[]{:S(2)}, u32[]{:S(2)}) collective-permute-start(bf16[1,32,256]{2,1,0:T(8,128)(2,1)S(1)} %get-tuple-element.41), channel_id=1, source_target_pairs={{1,0},{3,2},{5,4},{7,6},{9,8},{11,10},{13,12},{15,14},{17,16},{19,... | collective-permute-start | bytes 49160 | tf_op jit(solution)/shard_map/ppermute | solution.py:20
  42.1 11.1 %copy-start.4 = (bf16[256,128]{1,0:T(8,128)(2,1)}, bf16[256,128]{1,0:T(8,128)(2,1)S(1)}, u32[]{:S(2)}) copy-start(bf16[256,128]{1,0:T(8,128)(2,1)S(1)} %fusion.25) | copy-start | bytes 196612
  42.1 9.1 %collective-permute-start.4 = (bf16[1,32,256]{2,1,0:T(8,128)(2,1)S(1)}, bf16[1,32,256]{2,1,0:T(8,128)(2,1)S(1)}, u32[]{:S(2)}, u32[]{:S(2)}) collective-permute-start(bf16[1,32,256]{2,1,0:T(8,128)(2,1)S(1)} %get-tuple-element.38), channel_id=1, source_target_pairs={{0,1},{2,3},{4,5},{6,7},{8,9},{10,11},{12,13},{14,15},{16,17},{18,... | collective-permute-start | bytes 49160 | tf_op jit(solution)/shard_map/ppermute | solution.py:19
  44.2 7.0 %collective-permute-start.5 = (bf16[1,32,256]{2,1,0:T(8,128)(2,1)S(1)}, bf16[1,32,256]{2,1,0:T(8,128)(2,1)S(1)}, u32[]{:S(2)}, u32[]{:S(2)}) collective-permute-start(bf16[1,32,256]{2,1,0:T(8,128)(2,1)S(1)} %get-tuple-element.39), channel_id=1, source_target_pairs={{1,0},{3,2},{5,4},{7,6},{9,8},{11,10},{13,12},{15,14},{17,16},{19,... | collective-permute-start | bytes 49160 | tf_op jit(solution)/shard_map/ppermute | solution.py:20
  45.5 12.4 %all-to-all-start.1 = ((bf16[1,8,64]{2,0,1:T(2,128)(2,1)}), bf16[1,8,64]{2,0,1:T(2,128)(2,1)S(1)}, u32[]{:S(2)}, u32[]{:S(2)}) async-start(bf16[1,8,64]{2,0,1:T(2,128)(2,1)} %convert_element_type.145), calls=%async_computation.1 | async-start | bytes 8192 | tf_op jit(solution)/shard_map/all_to_all | solution.py:120
  53.2 0.7 copy-start.6
  53.9 9.8 %collective-permute-start.6 = (bf16[1,32,256]{2,1,0:T(8,128)(2,1)S(1)}, bf16[1,32,256]{2,1,0:T(8,128)(2,1)S(1)}, u32[]{:S(2)}, u32[]{:S(2)}) collective-permute-start(bf16[1,32,256]{2,1,0:T(8,128)(2,1)S(1)} %get-tuple-element.36), channel_id=1, source_target_pairs={{0,1},{2,3},{4,5},{6,7},{8,9},{10,11},{12,13},{14,15},{16,17},{18,... | collective-permute-start | bytes 49160 | tf_op jit(solution)/shard_map/ppermute | solution.py:19
  56.6 7.1 %collective-permute-start.7 = (bf16[1,32,256]{2,1,0:T(8,128)(2,1)S(1)}, bf16[1,32,256]{2,1,0:T(8,128)(2,1)S(1)}, u32[]{:S(2)}, u32[]{:S(2)}) collective-permute-start(bf16[1,32,256]{2,1,0:T(8,128)(2,1)S(1)} %get-tuple-element.37), channel_id=1, source_target_pairs={{1,0},{3,2},{5,4},{7,6},{9,8},{11,10},{13,12},{15,14},{17,16},{19,... | collective-permute-start | bytes 49160 | tf_op jit(solution)/shard_map/ppermute | solution.py:20
  58.0 15.9 %all-to-all-start = ((bf16[1,8,64,256]{3,2,0,1:T(8,128)(2,1)}), bf16[1,8,64,256]{3,2,0,1:T(8,128)(2,1)S(1)}, u32[]{:S(2)}, u32[]{:S(2)}) async-start(bf16[1,8,64,256]{3,2,0,1:T(8,128)(2,1)} %bitcast.61), calls=%async_computation | async-start | bytes 524288 | tf_op jit(solution)/shard_map/all_to_all | solution.py:113
  65.5 8.3 %copy-start.12 = (bf16[256,256]{1,0:T(8,128)(2,1)S(1)}, bf16[256,256]{1,0:T(8,128)(2,1)}, u32[]{:S(2)}) copy-start(bf16[256,256]{1,0:T(8,128)(2,1)} %param.24) | copy-start | bytes 393220
  74.8 1.8 %copy-start.13 = (bf16[256,256]{1,0:T(8,128)(2,1)S(1)}, bf16[256,256]{1,0:T(8,128)(2,1)}, u32[]{:S(2)}) copy-start(bf16[256,256]{1,0:T(8,128)(2,1)} %param.25) | copy-start | bytes 393220
  83.0 2.8 %copy-start.14 = (bf16[256,256]{1,0:T(8,128)(2,1)S(1)}, bf16[256,256]{1,0:T(8,128)(2,1)}, u32[]{:S(2)}) copy-start(bf16[256,256]{1,0:T(8,128)(2,1)} %param.26) | copy-start | bytes 393220
  88.9 5.8 %copy-start.8 = (bf16[8,32,256]{2,1,0:T(8,128)(2,1)S(1)}, bf16[8,32,256]{2,1,0:T(8,128)(2,1)}, u32[]{:S(2)}) copy-start(bf16[8,32,256]{2,1,0:T(8,128)(2,1)} %get-tuple-element.8) | copy-start | bytes 393220
  90.1 5.6 %copy-start.5 = (bf16[256,128]{1,0:T(8,128)(2,1)S(1)}, bf16[256,128]{1,0:T(8,128)(2,1)}, u32[]{:S(2)}) copy-start(bf16[256,128]{1,0:T(8,128)(2,1)} %copy-done.4) | copy-start | bytes 196612
  90.1 5.6 %copy-start.7 = (f32[256,256]{1,0:T(8,128)S(1)}, f32[256,256]{1,0:T(8,128)}, u32[]{:S(2)}) copy-start(f32[256,256]{1,0:T(8,128)} %copy-done.6) | copy-start | bytes 786436
  90.1 5.6 %copy-start.16 = (f32[256,128]{1,0:T(8,128)S(1)}, f32[256,128]{1,0:T(8,128)}, u32[]{:S(2)}) copy-start(f32[256,128]{1,0:T(8,128)} %convolution_add_fusion.16) | copy-start | bytes 393220
  90.1 5.6 %copy-start.17 = (bf16[8,32,256]{2,1,0:T(8,128)(2,1)S(1)}, bf16[8,32,256]{2,1,0:T(8,128)(2,1)}, u32[]{:S(2)}) copy-start(bf16[8,32,256]{2,1,0:T(8,128)(2,1)} %get-tuple-element.28) | copy-start | bytes 393220
  90.1 13.7 %copy-start.15 = (bf16[256,256]{1,0:T(8,128)(2,1)S(1)}, bf16[256,256]{1,0:T(8,128)(2,1)}, u32[]{:S(2)}) copy-start(bf16[256,256]{1,0:T(8,128)(2,1)} %param.27) | copy-start | bytes 393220
  91.0 12.8 %all-to-all-start.3 = ((bf16[8,1,64,256]{3,2,1,0:T(8,128)(2,1)}), bf16[8,1,64,256]{3,2,1,0:T(8,128)(2,1)S(1)}, u32[]{:S(2)}, u32[]{:S(2)}) async-start(bf16[8,1,64,256]{3,2,1,0:T(8,128)(2,1)} %copy.76), calls=%async_computation.3 | async-start | bytes 524288 | tf_op jit(solution)/shard_map/all_to_all | solution.py:155
where the time goes:
time: 107 us; the launch traced here: 106 us
  starting transfers between devices  37.2 us (35%)
  matrix products  24.6 us (23%)
  local copies, waits for them, and re-layouts  16.6 us (16%)
  waiting for transfers between devices  14.3 us (13%)
  blocking collectives  6.35 us (6%)
  other arithmetic  5.05 us (5%)
  between operations  1.63 us (2%)
    ppermute x4, starting transfers between devices, with_halo(): before = lax.ppermute(last, axis, up)  9.94 us
    dot_general x36, matrix products, conv_rows(): jnp.dot(window.reshape(rows * columns, -1), weight[row_shift, col_shift],...  9.4 us
    all_to_all x1, starting transfers between devices, on_device(): lax.all_to_all(anchor_split, 'frame', split_axis=1, concat_axis=0, tiled=...  6.98 us
    all_to_all x1, waiting for transfers between devices, on_device(): lax.all_to_all(local_tokens.reshape(1, frames, per_device, channels), 'fr...  6.77 us
    all_to_all x1, waiting for transfers between devices, on_device(): lax.all_to_all(track_result, 'frame', split_axis=0, concat_axis=1, tiled=...  6.47 us
    all_to_all x1, starting transfers between devices, on_device(): lax.all_to_all(local_tokens.reshape(1, frames, per_device, channels), 'fr...  5.72 us
    all_to_all x1, starting transfers between devices, on_device(): lax.all_to_all(seen_split, 'frame', split_axis=1, concat_axis=0, tiled=True)  5.72 us
    ppermute x4, starting transfers between devices, with_halo(): after = lax.ppermute(first, axis, down)  5.17 us
  transfers between devices with their start and end apart: 12, of which 3 were waited for; matrix products, arithmetic and copies ran while one was open for 12% of the time, Pallas kernels for 0%

commit v1 on v0

v1 whole, which is shorter than its diff:
```python
import math

import jax
import jax.numpy as jnp
from jax import lax
from jax.experimental import pallas as pl
from jax.experimental.pallas import tpu as pltpu
from jax.sharding import PartitionSpec as P

HEADS = 8
HEAD_DIM = 32
GRU_WIDTH = 128
ITERS = 2
LOGIT_SCALE = HEAD_DIM ** (-0.5) * math.log2(math.e)
MASKED = -1e30
GROUP = 16
MESH = pl.DeviceIdType.MESH
F32 = jnp.float32
BF16 = jnp.bfloat16
N_IN = 15


def dot(a, b):
    return jnp.dot(a, b, preferred_element_type=F32)


def dot_nt(a, b):
    return lax.dot_general(a, b, (((1,), (1,)), ((), ())), preferred_element_type=F32)


def iota(shape, dim):
    return lax.broadcasted_iota(jnp.int32, shape, dim)


def softmax_rows(scores, bias):
    scores = scores * LOGIT_SCALE + bias
    top = jnp.max(scores, axis=-1, keepdims=True)
    powers = jnp.exp2(scores - top)
    total = jnp.sum(powers, axis=-1, keepdims=True)
    return (powers * (1.0 / total)).astype(BF16)


def column_taps(x, columns):
    length = x.shape[0]
    col = lax.rem(iota(x.shape, 0), columns)
    left = jnp.where(col == 0, 0.0, pltpu.roll(x, 1, 0))
    right = jnp.where(col == columns - 1, 0.0, pltpu.roll(x, length - 1, 0))
    return jnp.concatenate([left.astype(BF16), x.astype(BF16), right.astype(BF16)], axis=1)


def interior_conv(x, w_ref, low, columns):
    width = x.shape[1]
    taps = column_taps(x, columns)
    zero = jnp.zeros((columns, taps.shape[1]), BF16)
    above = jnp.concatenate([zero, taps[:-columns]], axis=0)
    below = jnp.concatenate([taps[columns:], zero], axis=0)
    patches = jnp.concatenate([above, taps, below], axis=1)
    weight = w_ref[:, :, low : low + width, :]
    return dot(patches, weight.reshape(9 * width, weight.shape[3]))


def kernel(frames, bands, *refs):
    inputs, refs = refs[:N_IN], refs[N_IN:]
    (out_state, out_track), refs = refs[:2], refs[2:]
    held, refs = refs[:N_IN], refs[N_IN:]
    (
        partner_tok,
        partner_vis,
        tok_all,
        vis_all,
        keys,
        values,
        t_q,
        t_k,
        t_v,
        att_out,
        returned,
        stages,
        halos,
        attended,
        acc_g,
        acc_c,
        ctx_g,
        ctx_c,
        in_sem,
        own_sem,
        partner_send,
        partner_recv,
        tok_send,
        tok_recv,
        vis_send,
        vis_recv,
        back_send,
        back_recv,
        halo_send,
        halo_recv,
    ) = refs
    (pix_h, gst_h, tok_h, vis_h) = inputs[:4]
    (pix, gst, tok, vis, qfr, wpq, wpk, wpv, wpo, wtq, wtk, wtv, wto, wg, wc) = held
    me = lax.axis_index("frame")
    band = lax.axis_index("band")
    other = lax.rem(band + 1, bands)
    tracks, channels = tok.shape[1], tok.shape[2]
    mine = tracks // frames
    rows, columns = pix.shape[1], pix.shape[2]
    pixels = rows * columns

    loads = [pltpu.make_async_copy(inputs[i], held[i], in_sem.at[i]) for i in range(N_IN)]
    for i in (2, 6, 7, 0, 5, 3, 4, 9, 10, 11, 8, 1, 13, 14, 12):
        loads[i].start()

    barrier = pltpu.get_barrier_semaphore()
    for k in range(1, frames):
        pl.semaphore_signal(
            barrier, inc=1, device_id={"frame": lax.rem(me + k, frames)}, device_id_type=MESH
        )
    pl.semaphore_signal(barrier, inc=1, device_id={"band": other}, device_id_type=MESH)
    pl.semaphore_wait(barrier, frames)

    def to_partner(src, dst, send, recv):
        return pltpu.make_async_remote_copy(
            src_ref=src,
            dst_ref=dst,
            send_sem=send,
            recv_sem=recv,
            device_id={"band": other},
            device_id_type=MESH,
        )

    def to_frame(k, src, dst, send, recv):
        return pltpu.make_async_remote_copy(
            src_ref=src,
            dst_ref=dst,
            send_sem=send.at[k],
            recv_sem=recv.at[k],
            device_id={"frame": lax.rem(me + k, frames)},
            device_id_type=MESH,
        )

    partner_copies = [
        to_partner(tok_h.at[0], partner_tok, partner_send.at[0], partner_recv.at[0]),
        to_partner(vis_h, partner_vis, partner_send.at[1], partner_recv.at[1]),
    ]
    edge_row = (1 - band) * (rows - 1)
    edge = pl.multiple_of(edge_row * columns, columns)
    halo_copies = [
        to_partner(gst_h.at[0, edge_row], halos.at[0], halo_send.at[0], halo_recv.at[0])
    ]
    for copy in partner_copies:
        copy.start()
    frame_copies = []
    for k in range(1, frames):
        target = lax.rem(me + k, frames)
        frame_copies.append(
            to_frame(
                k,
                tok_h.at[0, pl.ds(pl.multiple_of(target * mine, mine), mine)],
                tok_all.at[me],
                tok_send,
                tok_recv,
            )
        )
        frame_copies.append(to_frame(k, vis_h, vis_all.at[me], vis_send, vis_recv))
    for copy in frame_copies:
        copy.start()
    own_copies = [
        pltpu.make_async_copy(
            tok_h.at[0, pl.ds(pl.multiple_of(me * mine, mine), mine)],
            tok_all.at[me],
            own_sem.at[0],
        ),
        pltpu.make_async_copy(vis_h, vis_all.at[me], own_sem.at[1]),
    ]
    for copy in own_copies:
        copy.start()
    halo_copies[0].start()

    for i in (2, 6, 7):
        loads[i].wait()
    keys[0:tracks, :] = dot(tok[0], wpk[...]).astype(BF16)
    values[0:tracks, :] = dot(tok[0], wpv[...]).astype(BF16)
    for i in (0, 5, 3):
        loads[i].wait()
    queries = dot(pix[0].reshape(pixels, channels), wpq[...]).astype(BF16)
    for copy in partner_copies:
        copy.wait_recv()
    keys[tracks:, :] = dot(partner_tok[...], wpk[...]).astype(BF16)
    values[tracks:, :] = dot(partner_tok[...], wpv[...]).astype(BF16)
    seen = jnp.concatenate([vis[...], partner_vis[...]], axis=1)
    pixel_bias = jnp.where(seen > 0, 0.0, MASKED)
    lane_head = lax.div(iota((1, channels), 1), HEAD_DIM)
    attended[...] = jnp.zeros_like(attended)

    def pixel_head(h, carry):
        chosen = jnp.where(lane_head == h, 1.0, 0.0)
        weights = softmax_rows(dot_nt(queries * chosen.astype(BF16), keys[...]), pixel_bias)
        attended[...] += dot(weights, values[...]) * chosen
        return carry

    lax.fori_loop(0, HEADS, pixel_head, 0)
    loads[8].wait()
    context = dot(attended[...].astype(BF16), wpo[...]).astype(BF16)

    def share_edge(stage, value):
        stages[stage - 1, :, :] = value
        copy = to_partner(
            stages.at[stage - 1, pl.ds(edge, columns)],
            halos.at[stage],
            halo_send.at[stage],
            halo_recv.at[stage],
        )
        copy.start()
        halo_copies.append(copy)

    share_edge(1, context)

    for i in (4, 9, 10, 11):
        loads[i].wait()
    for copy in own_copies:
        copy.wait()
    for copy in frame_copies:
        copy.wait_recv()
    block = frames * GROUP
    flat = tok_all[...].reshape(frames * mine, channels)
    for weight, dst in ((wtq, t_q), (wtk, t_k), (wtv, t_v)):
        dst[...] = dot(flat, weight[...]).astype(BF16).reshape(frames, mine, channels)
    picked_shape = (tracks, frames * mine)
    slot = iota(picked_shape, 1)
    picked = me * mine + lax.div(slot, block) * GROUP + lax.rem(slot, GROUP)
    pick = jnp.where(iota(picked_shape, 0) == picked, 1.0, 0.0).astype(BF16)
    slot_frame = lax.rem(lax.div(iota((frames, frames * mine), 1), GROUP), frames)
    vis_rows = dot(vis_all[...].reshape(frames, tracks).astype(F32).astype(BF16), pick)
    vis_row = jnp.sum(
        jnp.where(slot_frame == iota(slot_frame.shape, 0), vis_rows, 0.0), axis=0, keepdims=True
    )
    query_rows = jnp.broadcast_to(qfr[...].astype(F32), (GROUP, tracks)).astype(BF16)
    query_row = dot(query_rows, pick)[0:1]
    same = lax.rem(iota((block, block), 0), GROUP) == lax.rem(iota((block, block), 1), GROUP)
    key_frame = lax.div(iota((block, block), 1), GROUP).astype(F32)
    together = max(1, min(HEADS, 1024 // block))
    for g in range(mine // GROUP):
        part = slice(g * GROUP, (g + 1) * GROUP)
        cols = slice(g * block, (g + 1) * block)
        q_g = t_q[:, part, :].reshape(block, channels)
        k_g = t_k[:, part, :].reshape(block, channels)
        v_g = t_v[:, part, :].reshape(block, channels)
        is_anchor = jnp.logical_and(same, key_frame == query_row[:, cols])
        anchor = dot(jnp.where(is_anchor, 1.0, 0.0).astype(BF16), q_g)
        joint = (q_g.astype(F32) + anchor).astype(BF16)
        allowed = jnp.logical_and(same, vis_row[:, cols] > 0.5)
        bias = jnp.where(allowed, 0.0, MASKED)
        biases = jnp.concatenate([bias] * together, axis=0)
        result = jnp.zeros((block, channels), F32)
        for first in range(0, HEADS, together):
            masks = [
                jnp.where(lane_head == first + h, 1.0, 0.0) for h in range(together)
            ]
            stacked = jnp.concatenate([joint * m.astype(BF16) for m in masks], axis=0)
            weights = softmax_rows(dot_nt(stacked, k_g), biases)
            mixed = dot(weights, v_g)
            for h in range(together):
                result = result + mixed[h * block : (h + 1) * block] * masks[h]
        att_out[:, part, :] = result.astype(BF16).reshape(frames, GROUP, channels)
    back_copies = []
    for k in range(1, frames):
        target = lax.rem(me + k, frames)
        back_copies.append(
            to_frame(k, att_out.at[target], returned.at[me], back_send, back_recv)
        )
    for copy in back_copies:
        copy.start()
    returned[pl.ds(me, 1)] = att_out[pl.ds(me, 1)]

    def add_halo(acc, stage, w_ref, low):
        taps = column_taps(halos[stage].astype(F32), columns)
        weight = w_ref[pl.ds((1 - band) * 2, 1), :, low : low + GRU_WIDTH, :]
        weight = weight.reshape(3 * GRU_WIDTH, weight.shape[3])
        acc[pl.ds(edge, columns), :] += dot(taps, weight)

    for i in (1, 13, 14):
        loads[i].wait()
    context_f32 = context.astype(F32)
    ctx_g[...] = interior_conv(context_f32, wg, GRU_WIDTH, columns)
    ctx_c[...] = interior_conv(context_f32, wc, GRU_WIDTH, columns)
    halo_copies[1].wait_recv()
    add_halo(ctx_g, 1, wg, GRU_WIDTH)
    add_halo(ctx_c, 1, wc, GRU_WIDTH)
    state = gst[0].reshape(pixels, GRU_WIDTH).astype(F32)
    state_stage = 0
    for iteration in range(ITERS):
        acc_g[...] = ctx_g[...] + interior_conv(state, wg, 0, columns)
        halo_copies[state_stage].wait_recv()
        add_halo(acc_g, state_stage, wg, 0)
        reset = jax.nn.sigmoid(acc_g[:, GRU_WIDTH:])
        reset_state = (reset * state).astype(BF16)
        share_edge(2 + 2 * iteration, reset_state)
        update = jax.nn.sigmoid(acc_g[:, :GRU_WIDTH])
        acc_c[...] = ctx_c[...] + interior_conv(reset_state.astype(F32), wc, 0, columns)
        halo_copies[2 + 2 * iteration].wait_recv()
        add_halo(acc_c, 2 + 2 * iteration, wc, 0)
        candidate = jnp.tanh(acc_c[...])
        new_state = ((1.0 - update) * state + update * candidate).astype(BF16)
        if iteration < ITERS - 1:
            state_stage = 3 + 2 * iteration
            share_edge(state_stage, new_state)
            state = new_state.astype(F32)
    out_state[...] = new_state.reshape(1, rows, columns, GRU_WIDTH)

    loads[12].wait()
    for copy in back_copies:
        copy.wait_recv()
    track_update = dot(returned[...].reshape(tracks, channels), wto[...])
    out_track[0] = (tok[0].astype(F32) + track_update).astype(BF16)
    for copy in partner_copies + frame_copies + back_copies + halo_copies:
        copy.wait_send()


def on_device(frames, bands, *args):
    args = list(args)
    args[4] = args[4].reshape(1, -1)
    pixels, gru_state, tokens, visible = args[:4]
    tracks, channels = tokens.shape[1:]
    mine = tracks // frames
    rows, columns = pixels.shape[1:3]
    count = rows * columns
    halo_stages = 1 + 2 * ITERS
    dma = pltpu.SemaphoreType.DMA
    scratch = [pltpu.VMEM(a.shape, a.dtype) for a in args] + [
        pltpu.VMEM((tracks, channels), BF16),
        pltpu.VMEM((1, tracks), jnp.int32),
        pltpu.VMEM((frames, mine, channels), BF16),
        pltpu.VMEM((frames, 1, tracks), jnp.int32),
        pltpu.VMEM((2 * tracks, channels), BF16),
        pltpu.VMEM((2 * tracks, channels), BF16),
        pltpu.VMEM((frames, mine, channels), BF16),
        pltpu.VMEM((frames, mine, channels), BF16),
        pltpu.VMEM((frames, mine, channels), BF16),
        pltpu.VMEM((frames, mine, channels), BF16),
        pltpu.VMEM((frames, mine, channels), BF16),
        pltpu.VMEM((halo_stages - 1, count, GRU_WIDTH), BF16),
        pltpu.VMEM((halo_stages, columns, GRU_WIDTH), BF16),
        pltpu.VMEM((count, channels), F32),
        pltpu.VMEM((count, 2 * GRU_WIDTH), F32),
        pltpu.VMEM((count, GRU_WIDTH), F32),
        pltpu.VMEM((count, 2 * GRU_WIDTH), F32),
        pltpu.VMEM((count, GRU_WIDTH), F32),
        dma((N_IN,)),
        dma((2,)),
        dma((2,)),
        dma((2,)),
        dma((frames,)),
        dma((frames,)),
        dma((frames,)),
        dma((frames,)),
        dma((frames,)),
        dma((frames,)),
        dma((halo_stages,)),
        dma((halo_stages,)),
    ]

    def body(*refs):
        kernel(frames, bands, *refs)

    return pl.pallas_call(
        body,
        out_shape=(
            jax.ShapeDtypeStruct(gru_state.shape, BF16),
            jax.ShapeDtypeStruct(tokens.shape, BF16),
        ),
        in_specs=[pl.BlockSpec(memory_space=pl.ANY)] * N_IN,
        out_specs=(pl.BlockSpec(memory_space=pltpu.VMEM),) * 2,
        scratch_shapes=scratch,
        compiler_params=pltpu.CompilerParams(collective_id=0, has_side_effects=True),
        name="track_step",
    )(*args)


def solution(mesh):
    frames, bands = mesh.shape["frame"], mesh.shape["band"]
    placed = (
        P(("clip", "frame"), "band", None, None),
        P(("clip", "frame"), "band", None, None),
        P(("clip", "frame"), "band", None),
        P(("clip", "frame"), "band"),
        P(("clip", "band")),
    ) + (P(),) * 10
    return jax.shard_map(
        lambda *args: on_device(frames, bands, *args),
        mesh=mesh,
        in_specs=placed,
        out_specs=(P(("clip", "frame"), "band", None, None), P(("clip", "frame"), "band", None)),
        check_vma=False,
    )
```

time: 107 us -> 30.7 us (0.29)
  starting transfers between devices: 37.2 us -> 0 us
  Pallas kernels: 0 us -> 26.7 us
  matrix products: 24.6 us -> 0 us
  waiting for transfers between devices: 14.3 us -> 0 us
  local copies, waits for them, and re-layouts: 16.6 us -> 3.14 us
  blocking collectives: 6.35 us -> 0 us
  other arithmetic: 5.05 us -> 0 us
    pallas_call x0 -> x1, Pallas kernels: none -> 26.7 us  [on_device(): pl.pallas_call(body, out_shape=(jax.ShapeDtypeStruct(gru_state.shape, BF1...]
    dot_general x62 -> x0, matrix products: 24.6 us -> none  [the longest x36 9.4 us: conv_rows(): jnp.dot(window.reshape(rows * columns, -1), weight[row_shift, col_shift],...]
    all_to_all x4 -> x0, starting transfers between devices: 22.1 us -> none  [the longest x1 6.98 us: on_device(): lax.all_to_all(anchor_split, 'frame', split_axis=1, concat_axis=0, tiled=...]
    ppermute x8 -> x0, starting transfers between devices: 15.1 us -> none  [the longest x4 9.94 us: with_halo(): before = lax.ppermute(last, axis, up)]
    all_to_all x4 -> x0, waiting for transfers between devices: 13.2 us -> none  [the longest x1 6.77 us: on_device(): lax.all_to_all(local_tokens.reshape(1, frames, per_device, channels), 'fr...]
    all_gather x3 -> x0, blocking collectives: 6.35 us -> none  [the longest x1 2.3 us: on_device(): lax.all_gather(key_local, 'band', axis=0, tiled=True)]
    another operation x5 -> x0, local copies, waits for them, and re-layouts: 5.9 us -> none  [the longest x2 2.98 us: temporal_core(): key_part.reshape(shaped)]
    convert_element_type x8 -> x0, local copies, waits for them, and re-layouts: 5.78 us -> none  [the longest x1 1.76 us: temporal_core(): (query_part.astype(jnp.float32) + anchor[None]).astype(jnp.bfloat16)]
  transfers between devices with their start and end apart: 12 -> 0, of which waited for: 3 -> 0; matrix products, arithmetic and copies ran while one was open for 12% -> 0% of each run, Pallas kernels for 0% -> 0%
where the time goes in v1:
time: 30.7 us; the launch traced here: 30.5 us
  Pallas kernels  26.7 us (87%)
  local copies, waits for them, and re-layouts  3.14 us (10%)
  between operations  0.64 us (2%)
    pallas_call x1, Pallas kernels, on_device(): pl.pallas_call(body, out_shape=(jax.ShapeDtypeStruct(gru_state.shape, BF1...  26.7 us
    unnamed x2, local copies, waits for them, and re-layouts  3.14 us

profile of v1, /device:TPU:0, one launch (start us, length us, event | category | flops | bytes accessed | tf_op | source)
XLA Modules:
  0.0 30.5 jit_solution(6140624821604525908)
XLA Ops:
  0.6 26.7 %track_step.1 = (bf16[1,8,32,128]{3,2,1,0:T(8,128)(2,1)}, bf16[1,512,256]{2,1,0:T(8,128)(2,1)}) custom-call(bf16[1,8,32,256]{3,2,1,0:T(8,128)(2,1)} %refs_0_.1, bf16[1,8,32,128]{3,2,1,0:T(8,128)(2,1)} %refs_1_.1, bf16[1,512,256]{2,1,0:T(8,128)(2,1)} %refs_2_.1, s32[1,512]{1,0:T(1,128)} %refs_3_.1, s32[1,512]{1,0:T(1,128)} %bitcast.1, ...), custom_call_target="tpu_custom_call" | custom-call | tf_op jit(solution)/shard_map/track_step/pallas_call | solution.py:364
  27.4 1.5 %copy.19 = bf16[1,8,32,128]{3,2,1,0:T(8,128)(2,1)} copy(bf16[1,8,32,128]{3,2,1,0:T(8,128)(2,1)} %get-tuple-element.4) | data formatting | bytes 131072
  28.8 1.7 %copy.20 = bf16[1,512,256]{2,1,0:T(8,128)(2,1)} copy(bf16[1,512,256]{2,1,0:T(8,128)(2,1)} %get-tuple-element.5) | data formatting | bytes 524288

commit v2 on v1

v2 whole, which is shorter than its diff:
```python
import math

import jax
import jax.numpy as jnp
from jax import lax
from jax.experimental import pallas as pl
from jax.experimental.pallas import tpu as pltpu
from jax.sharding import PartitionSpec as P

HEADS = 8
HEAD_DIM = 32
GRU_WIDTH = 128
ITERS = 2
LOGIT_SCALE = HEAD_DIM ** (-0.5) * math.log2(math.e)
MASKED = -1e30
GROUP = 16
MESH = pl.DeviceIdType.MESH
F32 = jnp.float32
BF16 = jnp.bfloat16
N_IN = 14
UNROLL = 4


def dot(a, b):
    return jnp.dot(a, b, preferred_element_type=F32)


def dot_nt(a, b):
    return lax.dot_general(a, b, (((1,), (1,)), ((), ())), preferred_element_type=F32)


def iota(shape, dim):
    return lax.broadcasted_iota(jnp.int32, shape, dim)


def softmax_rows(scores, bias):
    scores = scores * LOGIT_SCALE + bias
    top = jnp.max(scores, axis=-1, keepdims=True)
    powers = jnp.exp2(scores - top)
    total = jnp.sum(powers, axis=-1, keepdims=True)
    return (powers * (1.0 / total)).astype(BF16)


def column_taps(x, columns):
    length = x.shape[0]
    col = lax.rem(iota(x.shape, 0), columns)
    left = jnp.where(col == 0, 0.0, pltpu.roll(x, 1, 0))
    right = jnp.where(col == columns - 1, 0.0, pltpu.roll(x, length - 1, 0))
    return jnp.concatenate([left.astype(BF16), x.astype(BF16), right.astype(BF16)], axis=1)


def interior_conv(x, w_ref, low, columns):
    width = x.shape[1]
    taps = column_taps(x, columns)
    zero = jnp.zeros((columns, taps.shape[1]), BF16)
    above = jnp.concatenate([zero, taps[:-columns]], axis=0)
    below = jnp.concatenate([taps[columns:], zero], axis=0)
    patches = jnp.concatenate([above, taps, below], axis=1)
    weight = w_ref[:, :, low : low + width, :]
    return dot(patches, weight.reshape(9 * width, weight.shape[3]))


def kernel(frames, bands, *refs):
    inputs, refs = refs[:N_IN], refs[N_IN:]
    (out_state, returned), refs = refs[:2], refs[2:]
    held, refs = refs[:N_IN], refs[N_IN:]
    (
        partner_tok,
        partner_vis,
        tok_all,
        vis_all,
        queries,
        keys,
        values,
        att_out,
        stages,
        halos,
        attended,
        tops,
        totals,
        acc_g,
        acc_c,
        ctx_g,
        ctx_c,
        in_sem,
        own_sem,
        partner_send,
        partner_recv,
        tok_send,
        tok_recv,
        vis_send,
        vis_recv,
        back_send,
        back_recv,
        back_own,
        halo_send,
        halo_recv,
    ) = refs
    (pix_h, gst_h, tok_h, vis_h) = inputs[:4]
    (pix, gst, tok, vis, qfr, wpq, wpk, wpv, wpo, wtq, wtk, wtv, wg, wc) = held
    me = lax.axis_index("frame")
    band = lax.axis_index("band")
    other = lax.rem(band + 1, bands)
    tracks, channels = tok.shape[1], tok.shape[2]
    mine = tracks // frames
    chunks, part_rows = tok_all.shape[0], tok_all.shape[2]
    rows, columns = pix.shape[1], pix.shape[2]
    pixels = rows * columns

    loads = [pltpu.make_async_copy(inputs[i], held[i], in_sem.at[i]) for i in range(N_IN)]
    for i in (2, 6, 7, 0, 5, 3, 8, 4, 9, 10, 11, 1, 12, 13):
        loads[i].start()

    barrier = pltpu.get_barrier_semaphore()
    for k in range(1, frames):
        pl.semaphore_signal(
            barrier, inc=1, device_id={"frame": lax.rem(me + k, frames)}, device_id_type=MESH
        )
    pl.semaphore_signal(barrier, inc=1, device_id={"band": other}, device_id_type=MESH)

    for i in (2, 6, 7):
        loads[i].wait()
    lane_head = lax.div(iota((1, channels), 1), HEAD_DIM)
    attended[...] = jnp.zeros_like(attended)
    tops[...] = jnp.zeros_like(tops)
    totals[...] = jnp.zeros_like(totals)

    def attend_half(half, track_rows, seen):
        keys[...] = dot(track_rows, wpk[...]).astype(BF16)
        values[...] = dot(track_rows, wpv[...]).astype(BF16)
        bias = jnp.where(seen > 0, 0.0, MASKED)

        def pixel_head(h, carry):
            chosen = jnp.where(lane_head == h, 1.0, 0.0)
            scores = dot_nt(queries[...] * chosen.astype(BF16), keys[...])
            scores = scores * LOGIT_SCALE + bias
            top = jnp.max(scores, axis=-1, keepdims=True)
            powers = jnp.exp2(scores - top)
            total = jnp.sum(powers, axis=-1, keepdims=True)
            tops[half] += top * chosen
            totals[half] += total * chosen
            attended[half] += dot(powers.astype(BF16), values[...]) * chosen
            return carry

        lax.fori_loop(0, HEADS, pixel_head, 0, unroll=UNROLL)

    for i in (0, 5, 3):
        loads[i].wait()
    queries[...] = dot(pix[0].reshape(pixels, channels), wpq[...]).astype(BF16)
    attend_half(0, tok[0], vis[...])
    pl.semaphore_wait(barrier, frames)

    def to_partner(src, dst, send, recv):
        return pltpu.make_async_remote_copy(
            src_ref=src,
            dst_ref=dst,
            send_sem=send,
            recv_sem=recv,
            device_id={"band": other},
            device_id_type=MESH,
        )

    def to_frame(k, src, dst, send, recv):
        return pltpu.make_async_remote_copy(
            src_ref=src,
            dst_ref=dst,
            send_sem=send,
            recv_sem=recv,
            device_id={"frame": lax.rem(me + k, frames)},
            device_id_type=MESH,
        )

    partner_copies = [
        to_partner(tok_h.at[0], partner_tok, partner_send.at[0], partner_recv.at[0]),
        to_partner(vis_h, partner_vis, partner_send.at[1], partner_recv.at[1]),
    ]
    edge_row = (1 - band) * (rows - 1)
    edge = pl.multiple_of(edge_row * columns, columns)
    halo_copies = [
        to_partner(gst_h.at[0, edge_row], halos.at[0], halo_send.at[0], halo_recv.at[0])
    ]
    for copy in partner_copies:
        copy.start()
    order = sorted(range(1, frames), key=lambda k: -min(k, frames - k))
    vis_copies = [
        to_frame(k, vis_h, vis_all.at[me], vis_send.at[k], vis_recv.at[k]) for k in order
    ]
    tok_copies = []
    for c in range(chunks):
        for k in order:
            target = lax.rem(me + k, frames)
            start = pl.multiple_of(target * mine + c * part_rows, part_rows)
            tok_copies.append(
                to_frame(
                    k,
                    tok_h.at[0, pl.ds(start, part_rows)],
                    tok_all.at[c, me],
                    tok_send.at[c, k],
                    tok_recv.at[c, k],
                )
            )
    for copy in vis_copies + tok_copies:
        copy.start()
    own_copies = [
        pltpu.make_async_copy(
            tok_h.at[0, pl.ds(pl.multiple_of(me * mine + c * part_rows, part_rows), part_rows)],
            tok_all.at[c, me],
            own_sem.at[c],
        )
        for c in range(chunks)
    ]
    own_copies.append(pltpu.make_async_copy(vis_h, vis_all.at[me], own_sem.at[chunks]))
    for copy in own_copies:
        copy.start()
    halo_copies[0].start()

    for copy in partner_copies:
        copy.wait_recv()
    attend_half(1, partner_tok[...], partner_vis[...])
    highest = jnp.maximum(tops[0], tops[1])
    share_0 = jnp.exp2(tops[0] - highest)
    share_1 = jnp.exp2(tops[1] - highest)
    merged = (attended[0] * share_0 + attended[1] * share_1) / (
        totals[0] * share_0 + totals[1] * share_1
    )
    loads[8].wait()
    context = dot(merged.astype(BF16), wpo[...]).astype(BF16)

    def share_edge(stage, value):
        stages[stage - 1, :, :] = value
        copy = to_partner(
            stages.at[stage - 1, pl.ds(edge, columns)],
            halos.at[stage],
            halo_send.at[stage],
            halo_recv.at[stage],
        )
        copy.start()
        halo_copies.append(copy)

    share_edge(1, context)

    for i in (4, 9, 10, 11):
        loads[i].wait()
    for copy in own_copies:
        copy.wait()
    for copy in vis_copies:
        copy.wait_recv()
    block = frames * GROUP
    picked_shape = (tracks, frames * mine)
    slot = iota(picked_shape, 1)
    picked = me * mine + lax.div(slot, block) * GROUP + lax.rem(slot, GROUP)
    pick = jnp.where(iota(picked_shape, 0) == picked, 1.0, 0.0).astype(BF16)
    slot_frame = lax.rem(lax.div(iota((frames, frames * mine), 1), GROUP), frames)
    vis_rows = dot(vis_all[...].reshape(frames, tracks).astype(F32).astype(BF16), pick)
    vis_row = jnp.sum(
        jnp.where(slot_frame == iota(slot_frame.shape, 0), vis_rows, 0.0), axis=0, keepdims=True
    )
    query_rows = jnp.broadcast_to(qfr[...].astype(F32), (GROUP, tracks)).astype(BF16)
    query_row = dot(query_rows, pick)[0:1]
    same = lax.rem(iota((block, block), 0), GROUP) == lax.rem(iota((block, block), 1), GROUP)
    key_frame = lax.div(iota((block, block), 1), GROUP).astype(F32)
    together = max(1, min(HEADS, 1024 // block))
    back_copies = []
    own_back = []

    def attend_time(c):
        for copy in tok_copies[c * (frames - 1) : (c + 1) * (frames - 1)]:
            copy.wait_recv()
        flat = tok_all[c].reshape(frames * part_rows, channels)
        t_q, t_k, t_v = [
            dot(flat, weight[...]).astype(BF16).reshape(frames, part_rows, channels)
            for weight in (wtq, wtk, wtv)
        ]
        for g in range(part_rows // GROUP):
            part = slice(g * GROUP, (g + 1) * GROUP)
            first_col = (c * (part_rows // GROUP) + g) * block
            cols = slice(first_col, first_col + block)
            q_g = t_q[:, part, :].reshape(block, channels)
            k_g = t_k[:, part, :].reshape(block, channels)
            v_g = t_v[:, part, :].reshape(block, channels)
            is_anchor = jnp.logical_and(same, key_frame == query_row[:, cols])
            anchor = dot(jnp.where(is_anchor, 1.0, 0.0).astype(BF16), q_g)
            joint = (q_g.astype(F32) + anchor).astype(BF16)
            allowed = jnp.logical_and(same, vis_row[:, cols] > 0.5)
            bias = jnp.where(allowed, 0.0, MASKED)
            biases = jnp.concatenate([bias] * together, axis=0)
            result = jnp.zeros((block, channels), F32)
            for first in range(0, HEADS, together):
                masks = [jnp.where(lane_head == first + h, 1.0, 0.0) for h in range(together)]
                stacked = jnp.concatenate([joint * m.astype(BF16) for m in masks], axis=0)
                weights = softmax_rows(dot_nt(stacked, k_g), biases)
                mixed = dot(weights, v_g)
                for h in range(together):
                    result = result + mixed[h * block : (h + 1) * block] * masks[h]
            att_out[c, :, part, :] = result.astype(BF16).reshape(frames, GROUP, channels)
        there = pl.ds(c * part_rows, part_rows)
        for k in order:
            target = lax.rem(me + k, frames)
            copy = to_frame(
                k,
                att_out.at[c, target],
                returned.at[me, there],
                back_send.at[c, k],
                back_recv.at[c, k],
            )
            copy.start()
            back_copies.append(copy)
        copy = pltpu.make_async_copy(att_out.at[c, me], returned.at[me, there], back_own.at[c])
        copy.start()
        own_back.append(copy)

    attend_time(0)

    def add_halo(acc, stage, w_ref, low):
        taps = column_taps(halos[stage].astype(F32), columns)
        weight = w_ref[pl.ds((1 - band) * 2, 1), :, low : low + GRU_WIDTH, :]
        weight = weight.reshape(3 * GRU_WIDTH, weight.shape[3])
        acc[pl.ds(edge, columns), :] += dot(taps, weight)

    for i in (1, 12, 13):
        loads[i].wait()
    context_f32 = context.astype(F32)
    ctx_g[...] = interior_conv(context_f32, wg, GRU_WIDTH, columns)
    ctx_c[...] = interior_conv(context_f32, wc, GRU_WIDTH, columns)
    halo_copies[1].wait_recv()
    add_halo(ctx_g, 1, wg, GRU_WIDTH)
    add_halo(ctx_c, 1, wc, GRU_WIDTH)
    for c in range(1, chunks):
        attend_time(c)
    state = gst[0].reshape(pixels, GRU_WIDTH).astype(F32)
    state_stage = 0
    for iteration in range(ITERS):
        acc_g[...] = ctx_g[...] + interior_conv(state, wg, 0, columns)
        halo_copies[state_stage].wait_recv()
        add_halo(acc_g, state_stage, wg, 0)
        reset = jax.nn.sigmoid(acc_g[:, GRU_WIDTH:])
        reset_state = (reset * state).astype(BF16)
        share_edge(2 + 2 * iteration, reset_state)
        update = jax.nn.sigmoid(acc_g[:, :GRU_WIDTH])
        acc_c[...] = ctx_c[...] + interior_conv(reset_state.astype(F32), wc, 0, columns)
        halo_copies[2 + 2 * iteration].wait_recv()
        add_halo(acc_c, 2 + 2 * iteration, wc, 0)
        candidate = jnp.tanh(acc_c[...])
        new_state = ((1.0 - update) * state + update * candidate).astype(BF16)
        if iteration < ITERS - 1:
            state_stage = 3 + 2 * iteration
            share_edge(state_stage, new_state)
            state = new_state.astype(F32)
    out_state[...] = new_state.reshape(1, rows, columns, GRU_WIDTH)

    for copy in own_back:
        copy.wait()
    for copy in back_copies:
        copy.wait_recv()
    for copy in partner_copies + vis_copies + tok_copies + back_copies + halo_copies:
        copy.wait_send()


def finish(state, tok, returned, wto, out_state, out_track):
    out_state[...] = state[...]
    update = dot(returned[...].reshape(tok.shape[1], tok.shape[2]), wto[...])
    out_track[0] = (tok[0].astype(F32) + update).astype(BF16)


def on_device(frames, bands, *args):
    args = list(args)
    args[4] = args[4].reshape(1, -1)
    time_out = args.pop(12)
    pixels, gru_state, tokens, visible = args[:4]
    tracks, channels = tokens.shape[1:]
    mine = tracks // frames
    chunks = 2 if mine % (2 * GROUP) == 0 else 1
    part_rows = mine // chunks
    rows, columns = pixels.shape[1:3]
    count = rows * columns
    halo_stages = 1 + 2 * ITERS
    dma = pltpu.SemaphoreType.DMA
    scratch = [pltpu.VMEM(a.shape, a.dtype) for a in args] + [
        pltpu.VMEM((tracks, channels), BF16),
        pltpu.VMEM((1, tracks), jnp.int32),
        pltpu.VMEM((chunks, frames, part_rows, channels), BF16),
        pltpu.VMEM((frames, 1, tracks), jnp.int32),
        pltpu.VMEM((count, channels), BF16),
        pltpu.VMEM((tracks, channels), BF16),
        pltpu.VMEM((tracks, channels), BF16),
        pltpu.VMEM((chunks, frames, part_rows, channels), BF16),
        pltpu.VMEM((halo_stages - 1, count, GRU_WIDTH), BF16),
        pltpu.VMEM((halo_stages, columns, GRU_WIDTH), BF16),
        pltpu.VMEM((2, count, channels), F32),
        pltpu.VMEM((2, count, channels), F32),
        pltpu.VMEM((2, count, channels), F32),
        pltpu.VMEM((count, 2 * GRU_WIDTH), F32),
        pltpu.VMEM((count, GRU_WIDTH), F32),
        pltpu.VMEM((count, 2 * GRU_WIDTH), F32),
        pltpu.VMEM((count, GRU_WIDTH), F32),
        dma((N_IN,)),
        dma((chunks + 1,)),
        dma((2,)),
        dma((2,)),
        dma((chunks, frames)),
        dma((chunks, frames)),
        dma((frames,)),
        dma((frames,)),
        dma((chunks, frames)),
        dma((chunks, frames)),
        dma((chunks,)),
        dma((halo_stages,)),
        dma((halo_stages,)),
    ]

    def body(*refs):
        kernel(frames, bands, *refs)

    state, returned = pl.pallas_call(
        body,
        out_shape=(
            jax.ShapeDtypeStruct(gru_state.shape, BF16),
            jax.ShapeDtypeStruct((frames, mine, channels), BF16),
        ),
        in_specs=[pl.BlockSpec(memory_space=pl.ANY)] * N_IN,
        out_specs=(
            pl.BlockSpec(memory_space=pltpu.VMEM),
            pl.BlockSpec(memory_space=pl.ANY),
        ),
        scratch_shapes=scratch,
        compiler_params=pltpu.CompilerParams(collective_id=0, has_side_effects=True),
        name="track_step",
    )(*args)
    return pl.pallas_call(
        finish,
        out_shape=(
            jax.ShapeDtypeStruct(gru_state.shape, BF16),
            jax.ShapeDtypeStruct(tokens.shape, BF16),
        ),
        in_specs=[pl.BlockSpec(memory_space=pltpu.VMEM)] * 4,
        out_specs=(pl.BlockSpec(memory_space=pltpu.VMEM),) * 2,
        name="track_finish",
    )(state, tokens, returned, time_out)


def solution(mesh):
    frames, bands = mesh.shape["frame"], mesh.shape["band"]
    placed = (
        P(("clip", "frame"), "band", None, None),
        P(("clip", "frame"), "band", None, None),
        P(("clip", "frame"), "band", None),
        P(("clip", "frame"), "band"),
        P(("clip", "band")),
    ) + (P(),) * 10
    return jax.shard_map(
        lambda *args: on_device(frames, bands, *args),
        mesh=mesh,
        in_specs=placed,
        out_specs=(P(("clip", "frame"), "band", None, None), P(("clip", "frame"), "band", None)),
        check_vma=False,
    )
```

time: 30.7 us -> 27.2 us (0.89)
  local copies, waits for them, and re-layouts: 3.14 us -> 0 us
    unnamed x2 -> x0, local copies, waits for them, and re-layouts: 3.14 us -> none
    pallas_call x1, Pallas kernels: 26.7 us -> 24.4 us  [on_device(): pl.pallas_call(body, out_shape=(jax.ShapeDtypeStruct(gru_state.shape, BF1...]
    pallas_call x0 -> x1, Pallas kernels: none -> 2.02 us  [on_device(): pl.pallas_call(finish, out_shape=(jax.ShapeDtypeStruct(gru_state.shape, B...]
where the time goes in v2:
time: 27.2 us; the launch traced here: 27 us
  Pallas kernels  26.4 us (97%)
  between operations  0.64 us (2%)
    pallas_call x1, Pallas kernels, on_device(): pl.pallas_call(body, out_shape=(jax.ShapeDtypeStruct(gru_state.shape, BF1...  24.4 us
    pallas_call x1, Pallas kernels, on_device(): pl.pallas_call(finish, out_shape=(jax.ShapeDtypeStruct(gru_state.shape, B...  2.02 us

profile of v2, /device:TPU:0, one launch (start us, length us, event | category | flops | bytes accessed | tf_op | source)
XLA Modules:
  0.0 27.0 jit_solution(16577586664996609600)
XLA Ops:
  0.6 24.4 %track_step.1 = (bf16[1,8,32,128]{3,2,1,0:T(8,128)(2,1)}, bf16[8,64,256]{2,1,0:T(8,128)(2,1)}) custom-call(bf16[1,8,32,256]{3,2,1,0:T(8,128)(2,1)} %refs_0_.1, bf16[1,8,32,128]{3,2,1,0:T(8,128)(2,1)} %refs_1_.1, bf16[1,512,256]{2,1,0:T(8,128)(2,1)} %tok.1, s32[1,512]{1,0:T(1,128)} %refs_3_.1, s32[1,512]{1,0:T(1,128)} %bitcast.1, bf16[256,256]{1,0:T(8,128)(2,1)} %refs_5_.1, ...), custom_call_target="tpu_custom_call" | custom-call | tf_op jit(solution)/shard_map/track_step/pallas_call | solution.py:414
  25.0 2.0 %track_finish.1 = (bf16[1,8,32,128]{3,2,1,0:T(8,128)(2,1)}, bf16[1,512,256]{2,1,0:T(8,128)(2,1)}) custom-call(bf16[1,8,32,128]{3,2,1,0:T(8,128)(2,1)} %get-tuple-element.4.state, bf16[1,512,256]{2,1,0:T(8,128)(2,1)} %tok.1, bf16[8,64,256]{2,1,0:T(8,128)(2,1)} %get-tuple-element.5.returned, bf16[256,256]{1,0:T(8,128)(2,1)} %wto.1), custom_call_target="tpu_custom_call" | custom-call | tf_op jit(solution)/shard_map/track_finish/pallas_call | solution.py:429

commit v3 on v2

--- a/solution.py
+++ b/solution.py
@@ -19,6 +19,7 @@
 BF16 = jnp.bfloat16
 N_IN = 14
 UNROLL = 4
+BEFORE = 4
 
 
 def dot(a, b):
@@ -125,7 +126,7 @@
     tops[...] = jnp.zeros_like(tops)
     totals[...] = jnp.zeros_like(totals)
 
-    def attend_half(half, track_rows, seen):
+    def attend_half(half, track_rows, seen, middle=None):
         keys[...] = dot(track_rows, wpk[...]).astype(BF16)
         values[...] = dot(track_rows, wpv[...]).astype(BF16)
         bias = jnp.where(seen > 0, 0.0, MASKED)
@@ -142,13 +143,16 @@
             attended[half] += dot(powers.astype(BF16), values[...]) * chosen
             return carry
 
-        lax.fori_loop(0, HEADS, pixel_head, 0, unroll=UNROLL)
+        if middle is None:
+            lax.fori_loop(0, HEADS, pixel_head, 0, unroll=UNROLL)
+        else:
+            lax.fori_loop(0, BEFORE, pixel_head, 0, unroll=UNROLL)
+            middle()
+            lax.fori_loop(BEFORE, HEADS, pixel_head, 0, unroll=UNROLL)
 
     for i in (0, 5, 3):
         loads[i].wait()
     queries[...] = dot(pix[0].reshape(pixels, channels), wpq[...]).astype(BF16)
-    attend_half(0, tok[0], vis[...])
-    pl.semaphore_wait(barrier, frames)
 
     def to_partner(src, dst, send, recv):
         return pltpu.make_async_remote_copy(
@@ -179,8 +183,6 @@
     halo_copies = [
         to_partner(gst_h.at[0, edge_row], halos.at[0], halo_send.at[0], halo_recv.at[0])
     ]
-    for copy in partner_copies:
-        copy.start()
     order = sorted(range(1, frames), key=lambda k: -min(k, frames - k))
     vis_copies = [
         to_frame(k, vis_h, vis_all.at[me], vis_send.at[k], vis_recv.at[k]) for k in order
@@ -199,8 +201,6 @@
                     tok_recv.at[c, k],
                 )
             )
-    for copy in vis_copies + tok_copies:
-        copy.start()
     own_copies = [
         pltpu.make_async_copy(
             tok_h.at[0, pl.ds(pl.multiple_of(me * mine + c * part_rows, part_rows), part_rows)],
@@ -210,10 +210,19 @@
         for c in range(chunks)
     ]
     own_copies.append(pltpu.make_async_copy(vis_h, vis_all.at[me], own_sem.at[chunks]))
-    for copy in own_copies:
-        copy.start()
-    halo_copies[0].start()
-
+
+
+    def start_sends():
+        pl.semaphore_wait(barrier, frames)
+        for copy in partner_copies:
+            copy.start()
+        for copy in vis_copies + tok_copies:
+            copy.start()
+        for copy in own_copies:
+            copy.start()
+        halo_copies[0].start()
+
+    attend_half(0, tok[0], vis[...], start_sends)
     for copy in partner_copies:
         copy.wait_recv()
     attend_half(1, partner_tok[...], partner_vis[...])
@@ -309,7 +318,8 @@
         copy.start()
         own_back.append(copy)
 
-    attend_time(0)
+    for c in range(chunks):
+        attend_time(c)
 
     def add_halo(acc, stage, w_ref, low):
         taps = column_taps(halos[stage].astype(F32), columns)
@@ -325,8 +335,6 @@
     halo_copies[1].wait_recv()
     add_halo(ctx_g, 1, wg, GRU_WIDTH)
     add_halo(ctx_c, 1, wc, GRU_WIDTH)
-    for c in range(1, chunks):
-        attend_time(c)
     state = gst[0].reshape(pixels, GRU_WIDTH).astype(F32)
     state_stage = 0
     for iteration in range(ITERS):

time: 27.2 us -> 26.4 us (0.971)
  Pallas kernels: 26.4 us -> 25.6 us
    pallas_call x1, Pallas kernels: 24.4 us -> 23.6 us  [on_device(): pl.pallas_call(body, out_shape=(jax.ShapeDtypeStruct(gru_state.shape, BF1...]
where the time goes in v3:
time: 26.4 us; the launch traced here: 26.3 us
  Pallas kernels  25.6 us (97%)
  between operations  0.64 us (2%)
    pallas_call x1, Pallas kernels, on_device(): pl.pallas_call(body, out_shape=(jax.ShapeDtypeStruct(gru_state.shape, BF1...  23.6 us
    pallas_call x1, Pallas kernels, on_device(): pl.pallas_call(finish, out_shape=(jax.ShapeDtypeStruct(gru_state.shape, B...  2.03 us

profile of v3, /device:TPU:0, one launch (start us, length us, event | category | flops | bytes accessed | tf_op | source)
XLA Modules:
  0.0 26.3 jit_solution(1034445344104575898)
XLA Ops:
  0.6 23.6 %track_step.1 = (bf16[1,8,32,128]{3,2,1,0:T(8,128)(2,1)}, bf16[8,64,256]{2,1,0:T(8,128)(2,1)}) custom-call(bf16[1,8,32,256]{3,2,1,0:T(8,128)(2,1)} %refs_0_.1, bf16[1,8,32,128]{3,2,1,0:T(8,128)(2,1)} %refs_1_.1, bf16[1,512,256]{2,1,0:T(8,128)(2,1)} %tok.1, s32[1,512]{1,0:T(1,128)} %refs_3_.1, s32[1,512]{1,0:T(1,128)} %bitcast.1, bf16[256,256]{1,0:T(8,128)(2,1)} %refs_5_.1, ...), custom_call_target="tpu_custom_call" | custom-call | tf_op jit(solution)/shard_map/track_step/pallas_call | solution.py:422
  24.2 2.0 %track_finish.1 = (bf16[1,8,32,128]{3,2,1,0:T(8,128)(2,1)}, bf16[1,512,256]{2,1,0:T(8,128)(2,1)}) custom-call(bf16[1,8,32,128]{3,2,1,0:T(8,128)(2,1)} %get-tuple-element.4.state, bf16[1,512,256]{2,1,0:T(8,128)(2,1)} %tok.1, bf16[8,64,256]{2,1,0:T(8,128)(2,1)} %get-tuple-element.5.returned, bf16[256,256]{1,0:T(8,128)(2,1)} %wto.1), custom_call_target="tpu_custom_call" | custom-call | tf_op jit(solution)/shard_map/track_finish/pallas_call | solution.py:437
